TPU v7x, 128 devices: a whole 4x4x4 slice. The times are simulated.
128 devices in a mesh: gx: 8 (over x, core), gy: 4 (over z), band: 4 (over y).
Axes of the slice: x: 4, y: 4, z: 4, core: 2. Of those that a mesh axis runs over, the one named last changes fastest.
Arguments:
- block: float32 [32, 96, 18432], P('band', 'gx', 'gy'), may hold values from -9 to 9
- prior: float32 [256, 96, 18432], P('band', 'gx', 'gy'), may hold values from -9 to 9
- potential: float32 [96, 18432], P('gx', 'gy'), may hold values from -1.5 to 1
Outputs:
- orbitals: float32 [32, 96, 18432], P('band', 'gx', 'gy')
All inputs are finite; a program needn't handle non-finite values.
Results may differ from a plain program's by a relative error of at most 0.000098.
Values sent between devices are 32-bit elements; how exact they have to be, the bound alone decides.
A program may use at most 128 MiB of HBM per device.

v0:
```python
import jax
import jax.numpy as jnp
from jax import lax
from jax.sharding import PartitionSpec as P

NZ = 192
coeffs = (-205.0 / 72.0, 8.0 / 5.0, -1.0 / 5.0, 8.0 / 315.0, -1.0 / 560.0)


def extended_2(x, sides, width):
    for axis, dim in sides:
        devices, length = (lax.axis_size(axis), x.shape[dim])
        up = [(i, (i + 1) % devices) for i in range(devices - 1)]
        down = [(j, i) for i, j in up]
        last = lax.slice_in_dim(x, length - width, length, axis=dim)
        leading = lax.slice_in_dim(x, 0, width, axis=dim)
        before = lax.ppermute(last, axis, up)
        after = lax.ppermute(leading, axis, down)
        x = jnp.concatenate([before, x, after], axis=dim)
    return x


def laplace(padded):
    center = padded[:, 4:-4, 4:-4, 4:-4]
    total = 3.0 * coeffs[0] * center
    for shift in range(1, 5):
        total = total + coeffs[shift] * (
            padded[:, 4 + shift : padded.shape[1] - 4 + shift, 4:-4, 4:-4]
            + padded[:, 4 - shift : padded.shape[1] - 4 - shift, 4:-4, 4:-4]
        )
        total = total + coeffs[shift] * (
            padded[:, 4:-4, 4 + shift : padded.shape[2] - 4 + shift, 4:-4]
            + padded[:, 4:-4, 4 - shift : padded.shape[2] - 4 - shift, 4:-4]
        )
        total = total + coeffs[shift] * (
            padded[:, 4:-4, 4:-4, 4 + shift : padded.shape[3] - 4 + shift]
            + padded[:, 4:-4, 4:-4, 4 - shift : padded.shape[3] - 4 - shift]
        )
    return total


def matmul(left, right):
    return jnp.dot(left, right, precision=lax.Precision.HIGHEST, preferred_element_type=jnp.float32)


def shards(block, prior, potential):
    own_count = block.shape[0]
    rows_x = block.shape[1]
    rows_y = block.shape[2] // NZ
    total_count = own_count * lax.axis_size("band")
    ncells_all = rows_x * lax.axis_size("gx") * rows_y * lax.axis_size("gy") * NZ
    grid_block = block.reshape(own_count, rows_x, rows_y, NZ)
    extended = extended_2(grid_block, (("gx", 1), ("gy", 2)), 4)
    extended = jnp.pad(extended, ((0, 0), (0, 0), (0, 0), (4, 4)))
    lap_flat = laplace(extended).reshape(block.shape)
    phi = -2.0 * lap_flat + potential[None] * block
    phi_flat = phi.reshape(own_count, -1)
    prior_flat = prior.reshape(prior.shape[0], -1)
    phi_all = lax.all_gather(phi_flat, "band", axis=0, tiled=True)
    correlation = lax.psum(matmul(prior_flat, phi_all.T), ("gx", "gy")) / ncells_all
    removed = lax.psum_scatter(
        matmul(correlation.T, prior_flat), "band", scatter_dimension=0, tiled=True
    )
    projected_own = phi_flat - removed
    projected = lax.all_gather(projected_own, "band", axis=0, tiled=True)
    gram = lax.psum(matmul(projected, projected.T), ("gx", "gy")) / ncells_all
    lower = jnp.linalg.cholesky(gram)
    inverse = lax.linalg.triangular_solve(
        lower, jnp.eye(total_count, dtype=lower.dtype), left_side=True, lower=True
    )
    first_row = lax.axis_index("band") * own_count
    own_rows = lax.dynamic_slice_in_dim(inverse, first_row, own_count, 0)
    orbitals = matmul(own_rows, projected)
    return orbitals.reshape(block.shape)


def solution(mesh):
    in_specs = (P("band", "gx", "gy"), P("band", "gx", "gy"), P("gx", "gy"))
    out_specs = P("band", "gx", "gy")
    return jax.shard_map(shards, mesh=mesh, in_specs=in_specs, out_specs=out_specs, check_vma=False)
```

profile of v0, /device:TPU:0, one launch (start us, length us, event | category | flops | bytes accessed | tf_op | source)
XLA Modules:
  0.0 602.9 jit_solution(7956143481172874915)
XLA Ops:
  6.5 2.0 reshape.25
  8.7 1.3 collective-permute-start.1
  10.0 1.3 collective-permute-start
  12.9 3.1 collective-permute-done
  17.7 4.6 collective-permute-start.3
  22.3 6.6 %collective-permute-done.2 = f32[8,20,4,192]{3,2,0,1:T(4,128)S(1)} collective-permute-done((f32[8,20,4,192]{3,2,0,1:T(4,128)S(1)}, f32[8,20,4,192]{3,2,0,1:T(4,128)S(1)}, u32[]{:S(2)}, u32[]{:S(2)}) %collective-permute-start.2) | collective-permute-done | bytes 491552 | tf_op jit(solution)/shard_map/ppermute | solution.py:18
  28.9 1.5 collective-permute-done.3
  30.3 2.9 select_maximum_fusion
  33.2 20.7 %fusion.9 = f32[8,12,24,192]{3,2,0,1:T(8,128)} fusion(f32[8,20,24,192]{3,2,0,1:T(8,128)} %copy-done.3, f32[8,20,4,192]{3,2,0,1:T(4,128)S(1)} %collective-permute-done.3, f32[8,20,4,192]{3,2,0,1:T(4,128)S(1)} %collective-permute-done.2, f32[8,20,32,200]{3,2,0,1:T(8,128)S(1)} %select_maximum_fusion, f32[8,16,24,192]{3,2,0,1:T(8,128)} %copy-done.1, ...), kind=kLoop, calls=%fused_computation.25 | loop fusion | flops 20348928 | bytes 35782656 | tf_op jit(solution)/shard_map/mul | solution.py:56
  53.9 2.3 mul.78
  56.2 2.4 multiply_add_fusion
  58.9 11.4 %copy.10 = f32[12,8,8,4608]{3,2,0,1:T(8,128)} copy(f32[12,8,8,4608]{3,2,1,0:T(8,128)} %bitcast.31) | data formatting | bytes 28311552 | tf_op jit(solution)/shard_map/reshape | solution.py:58
  70.3 79.2 %all-gather.3.cloned.1.call-done = f32[32,55296]{1,0:T(8,128)} async-done(((f32[8,55296]{1,0:T(8,128)}), f32[32,55296]{1,0:T(8,128)}) %all-gather.3.cloned.1.call-update) | async-done | bytes 7077904 | tf_op jit(solution)/shard_map/all_gather | solution.py:59
  149.5 14.5 %convolution_bitcast_fusion = f32[64,32]{0,1:T(8,128)S(1)} fusion(f32[32,55296]{1,0:T(8,128)} %all-gather.3.cloned.1.call-done, f32[64,55296]{1,0:T(8,128)} %bitcast.27), kind=kOutput, calls=%fused_computation.63 | convolution fusion | flops 1358954496 | bytes 21241856 | tf_op jit(solution)/shard_map/dot_general | solution.py:43
  164.0 128.3 %psum.14 = f32[64,32]{0,1:T(8,128)S(1)} all-reduce(f32[64,32]{0,1:T(8,128)S(1)} %convolution_bitcast_fusion), channel_id=1, replica_groups=mesh['gx'=8,'gy'=4,'band'=4] {'gx','gy'}, use_global_device_ids=true, to_apply=%region_0.1 | all-reduce | flops 2048 | bytes 16384 | tf_op jit(solution)/shard_map/psum | solution.py:60
  292.3 11.7 %fusion.40 = f32[32,55296]{1,0:T(8,128)} fusion(f32[64,55296]{1,0:T(8,128)} %bitcast.28, f32[64,32]{0,1:T(8,128)S(1)} %psum.14), kind=kOutput, calls=%fused_computation.78 | convolution fusion | flops 1358956544 | bytes 21241856 | tf_op jit(solution)/shard_map/dot_general | solution.py:43
  304.0 66.2 %reduce-scatter.2.cloned.1.call-done = f32[8,55296]{1,0:T(8,128)} async-done(((f32[32,55296]{1,0:T(8,128)}), f32[8,55296]{1,0:T(8,128)}) %reduce-scatter.2.cloned.1.call-update) | async-done | bytes 1769488 | tf_op jit(solution)/shard_map/reduce_scatter | solution.py:61
  370.3 2.9 sub.3
  373.1 72.1 %all-gather.5.cloned.1.call-done = f32[32,55296]{1,0:T(8,128)} async-done(((f32[8,55296]{1,0:T(8,128)}), f32[32,55296]{1,0:T(8,128)}) %all-gather.5.cloned.1.call-update) | async-done | bytes 7077904 | tf_op jit(solution)/shard_map/all_gather | solution.py:65
  445.3 9.1 %fusion.49 = f32[32,32]{0,1:T(8,128)S(1)} fusion(f32[32,55296]{1,0:T(8,128)} %all-gather.5.cloned.1.call-done), kind=kOutput, calls=%fused_computation.91 | convolution fusion | flops 679477248 | bytes 7081984 | tf_op jit(solution)/shard_map/dot_general | solution.py:43
  454.4 128.5 %psum.15 = f32[32,32]{0,1:T(8,128)S(1)} all-reduce(f32[32,32]{0,1:T(8,128)S(1)} %fusion.49), channel_id=1, replica_groups=mesh['gx'=8,'gy'=4,'band'=4] {'gx','gy'}, use_global_device_ids=true, to_apply=%region_2.3 | all-reduce | flops 1024 | bytes 8192 | tf_op jit(solution)/shard_map/psum | solution.py:66
  583.0 2.9 cholesky.17
  587.2 2.4 custom-call.6
  589.9 6.5 %fusion.43 = f32[8,55296]{1,0:T(8,128)} fusion(f32[32,55296]{1,0:T(8,128)} %all-gather.5.cloned.1.call-done, f32[32,32]{1,0:T(8,128)S(1)} %fusion.37, s32[]{:T(128)S(6)} %select_n.8), kind=kOutput, calls=%fused_computation.84 | convolution fusion | flops 169869312 | bytes 8851460 | tf_op jit(solution)/shard_map/dot_general | solution.py:43
  (32 shorter events, 5.3 us)
Async XLA Ops:
  6.5 142.9 %all-gather.3.cloned.1.call-start = ((), (), s32[]{:S(2)}) async-start(), calls=%async_computation.1 | async-start | bytes 8847360 | tf_op jit(solution)/shard_map/all_gather | solution.py:59
  8.5 3.5 copy-start.2
  8.7 3.2 collective-permute-start.1
  10.0 5.9 collective-permute-start
  12.9 3.5 copy-start.1
  16.1 17.1 %copy-start = (f32[8,16,24,192]{3,2,0,1:T(8,128)}, f32[8,16,24,192]{3,2,0,1:T(8,128)S(1)}, u32[]{:S(2)}) copy-start(f32[8,16,24,192]{3,2,0,1:T(8,128)S(1)} %get-tuple-element.12) | copy-start | bytes 7077892
  16.1 17.1 %copy-start.3 = (f32[8,20,24,192]{3,2,0,1:T(8,128)}, f32[8,20,24,192]{3,2,0,1:T(8,128)S(1)}, u32[]{:S(2)}) copy-start(f32[8,20,24,192]{3,2,0,1:T(8,128)S(1)} %get-tuple-element.13) | copy-start | bytes 8847364
  16.4 12.5 %collective-permute-start.2 = (f32[8,20,4,192]{3,2,0,1:T(4,128)S(1)}, f32[8,20,4,192]{3,2,0,1:T(4,128)S(1)}, u32[]{:S(2)}, u32[]{:S(2)}) collective-permute-start(f32[8,20,4,192]{3,2,0,1:T(4,128)S(1)} %get-tuple-element.5), channel_id=1, source_target_pairs={{4,0},{8,4},{12,8},{5,1},{9,5},{13,9},{6,2},{10,6},{14,10},{7,3},{... | collective-permute-start | bytes 1474568 | tf_op jit(solution)/shard_map/ppermute | solution.py:18
  17.7 12.6 %collective-permute-start.3 = (f32[8,20,4,192]{3,2,0,1:T(4,128)S(1)}, f32[8,20,4,192]{3,2,0,1:T(4,128)S(1)}, u32[]{:S(2)}, u32[]{:S(2)}) collective-permute-start(f32[8,20,4,192]{3,2,0,1:T(4,128)S(1)} %get-tuple-element.6), channel_id=1, source_target_pairs={{0,4},{4,8},{8,12},{1,5},{5,9},{9,13},{2,6},{6,10},{10,14},{3,7},{... | collective-permute-start | bytes 1474568 | tf_op jit(solution)/shard_map/ppermute | solution.py:17
  53.9 2.3 copy-start.5
  58.7 311.6 %reduce-scatter.2.cloned.1.call-start = ((), (), s32[]{:S(2)}) async-start(), calls=%async_computation.2 | async-start | bytes 8847360 | tf_op jit(solution)/shard_map/reduce_scatter | solution.py:61
  304.0 66.3 %copy-start.4 = (f32[8,12,4608]{2,0,1:T(8,128)S(1)}, f32[8,12,4608]{2,0,1:T(8,128)}, u32[]{:S(2)}) copy-start(f32[8,12,4608]{2,0,1:T(8,128)} %multiply_add_fusion) | copy-start | bytes 5308420
  304.0 141.3 %all-gather.5.cloned.1.call-start = ((), (), s32[]{:S(2)}) async-start(), calls=%async_computation.3 | async-start | bytes 8847360 | tf_op jit(solution)/shard_map/all_gather | solution.py:65
Sparse Core Ops, SparseCore 0:
  58.8 90.6 all-gather.2
  304.1 66.1 reduce-scatter.1
  373.3 71.9 all-gather.4
where the time goes:
time: 603 us
  blocking collectives  257 us (43%)
  waiting for transfers between devices  229 us (38%)
  matrix products  42 us (7%)
  other arithmetic  35.5 us (6%)
  local copies, waits for them, and re-layouts  17.2 us (3%)
  between operations  13.3 us (2%)
  starting transfers between devices  8.78 us (1%)
    psum x1, blocking collectives, shards(): gram = lax.psum(matmul(projected, projected.T), ('gx', 'gy')) / ncells_all  129 us
    psum x1, blocking collectives, shards(): lax.psum(matmul(prior_flat, phi_all.T), ('gx', 'gy')) / ncells_all  128 us
    all_gather x1, waiting for transfers between devices, shards(): phi_all = lax.all_gather(phi_flat, 'band', axis=0, tiled=True)  79.2 us
    all_gather x1, waiting for transfers between devices, shards(): projected = lax.all_gather(projected_own, 'band', axis=0, tiled=True)  72.1 us
    reduce_scatter x1, waiting for transfers between devices, shards(): lax.psum_scatter(matmul(correlation.T, prior_flat), 'band', scatter_dimen...  66.2 us
    dot_general x4, matrix products, matmul(): jnp.dot(left, right, precision=lax.Precision.HIGHEST, preferred_element_t...  41.8 us
    mul x1, other arithmetic, shards(): phi = -2.0 * lap_flat + potential[None] * block  20.7 us
  transfers between devices with their start and end apart: 7, of which 7 were waited for; matrix products, arithmetic and copies ran while one was open for 2% of the time, Pallas kernels for 0%

commit v1 on v0

--- a/solution.py
+++ b/solution.py
@@ -57,7 +57,7 @@
     phi_flat = phi.reshape(own_count, -1)
     prior_flat = prior.reshape(prior.shape[0], -1)
     phi_all = lax.all_gather(phi_flat, "band", axis=0, tiled=True)
-    correlation = lax.psum(matmul(prior_flat, phi_all.T), ("gx", "gy")) / ncells_all
+    correlation = lax.psum(lax.psum(matmul(prior_flat, phi_all.T), "gy"), "gx") / ncells_all
     removed = lax.psum_scatter(
         matmul(correlation.T, prior_flat), "band", scatter_dimension=0, tiled=True
     )

time: 603 us -> 516 us (0.86)
  blocking collectives: 257 us -> 169 us
    psum x1 -> x2, blocking collectives: 128 us -> 40.6 us  [the longest x1 23.5 us: shards(): lax.psum(lax.psum(matmul(prior_flat, phi_all.T), 'gy'), 'gx') / ncells_all]
where the time goes in v1:
time: 516 us
  waiting for transfers between devices  230 us (45%)
  blocking collectives  169 us (33%)
  matrix products  42 us (8%)
  other arithmetic  35.5 us (7%)
  local copies, waits for them, and re-layouts  17.2 us (3%)
  between operations  13.3 us (3%)
  starting transfers between devices  8.78 us (2%)
    psum x1, blocking collectives, shards(): gram = lax.psum(matmul(projected, projected.T), ('gx', 'gy')) / ncells_all  129 us
    all_gather x1, waiting for transfers between devices, shards(): phi_all = lax.all_gather(phi_flat, 'band', axis=0, tiled=True)  79.2 us
    all_gather x1, waiting for transfers between devices, shards(): projected = lax.all_gather(projected_own, 'band', axis=0, tiled=True)  72.1 us
    reduce_scatter x1, waiting for transfers between devices, shards(): lax.psum_scatter(matmul(correlation.T, prior_flat), 'band', scatter_dimen...  66.5 us
    dot_general x4, matrix products, matmul(): jnp.dot(left, right, precision=lax.Precision.HIGHEST, preferred_element_t...  41.8 us
    psum x1, blocking collectives, shards(): lax.psum(lax.psum(matmul(prior_flat, phi_all.T), 'gy'), 'gx') / ncells_all  23.5 us
    mul x1, other arithmetic, shards(): phi = -2.0 * lap_flat + potential[None] * block  20.6 us
    psum x1, blocking collectives, shards(): lax.psum(matmul(prior_flat, phi_all.T), 'gy')  17.1 us
  transfers between devices with their start and end apart: 7, of which 7 were waited for; matrix products, arithmetic and copies ran while one was open for 2% of the time, Pallas kernels for 0%

profile of v1, /device:TPU:0, one launch (start us, length us, event | category | flops | bytes accessed | tf_op | source)
XLA Modules:
  0.0 515.5 jit_solution(15253603519158927917)
XLA Ops:
  6.5 2.0 reshape.25
  8.7 1.3 collective-permute-start.1
  12.9 3.1 collective-permute-done
  17.7 4.6 collective-permute-start.3
  22.3 6.6 %collective-permute-done.2 = f32[8,20,4,192]{3,2,0,1:T(4,128)S(1)} collective-permute-done((f32[8,20,4,192]{3,2,0,1:T(4,128)S(1)}, f32[8,20,4,192]{3,2,0,1:T(4,128)S(1)}, u32[]{:S(2)}, u32[]{:S(2)}) %collective-permute-start.2) | collective-permute-done | bytes 491552 | tf_op jit(solution)/shard_map/ppermute | solution.py:18
  28.9 1.5 collective-permute-done.3
  30.3 2.9 select_maximum_fusion
  33.2 20.6 %fusion.9 = f32[8,12,24,192]{3,2,0,1:T(8,128)} fusion(f32[8,20,24,192]{3,2,0,1:T(8,128)} %copy-done.3, f32[8,20,4,192]{3,2,0,1:T(4,128)S(1)} %collective-permute-done.3, f32[8,20,4,192]{3,2,0,1:T(4,128)S(1)} %collective-permute-done.2, f32[8,20,32,200]{3,2,0,1:T(8,128)S(1)} %select_maximum_fusion, f32[8,16,24,192]{3,2,0,1:T(8,128)} %copy-done.1, ...), kind=kLoop, calls=%fused_computation.25 | loop fusion | flops 20348928 | bytes 35782656 | tf_op jit(solution)/shard_map/mul | solution.py:56
  53.9 2.3 mul.78
  56.2 2.4 multiply_add_fusion
  58.9 11.4 %copy.10 = f32[12,8,8,4608]{3,2,0,1:T(8,128)} copy(f32[12,8,8,4608]{3,2,1,0:T(8,128)} %bitcast.31) | data formatting | bytes 28311552 | tf_op jit(solution)/shard_map/reshape | solution.py:58
  70.2 79.2 %all-gather.3.cloned.1.call-done = f32[32,55296]{1,0:T(8,128)} async-done(((f32[8,55296]{1,0:T(8,128)}), f32[32,55296]{1,0:T(8,128)}) %all-gather.3.cloned.1.call-update) | async-done | bytes 7077904 | tf_op jit(solution)/shard_map/all_gather | solution.py:59
  149.4 14.5 %convolution_bitcast_fusion = f32[64,32]{0,1:T(8,128)S(1)} fusion(f32[32,55296]{1,0:T(8,128)} %all-gather.3.cloned.1.call-done, f32[64,55296]{1,0:T(8,128)} %bitcast.27), kind=kOutput, calls=%fused_computation.63 | convolution fusion | flops 1358954496 | bytes 21241856 | tf_op jit(solution)/shard_map/dot_general | solution.py:43
  164.0 17.1 %psum.21 = f32[64,32]{0,1:T(8,128)S(1)} all-reduce(f32[64,32]{0,1:T(8,128)S(1)} %convolution_bitcast_fusion), channel_id=1, replica_groups=mesh['gx'=8,'gy'=4,'band'=4] {'gy'}, use_global_device_ids=true, to_apply=%region_0.1 | all-reduce | flops 2048 | bytes 16384 | tf_op jit(solution)/shard_map/psum | solution.py:60
  181.1 23.5 %psum.22 = f32[64,32]{0,1:T(8,128)S(1)} all-reduce(f32[64,32]{0,1:T(8,128)S(1)} %psum.21), channel_id=1, replica_groups=mesh['gx'=8,'gy'=4,'band'=4] {'gx'}, use_global_device_ids=true, to_apply=%region_1.2 | all-reduce | flops 2048 | bytes 16384 | tf_op jit(solution)/shard_map/psum | solution.py:60
  204.6 11.7 %fusion.40 = f32[32,55296]{1,0:T(8,128)} fusion(f32[64,55296]{1,0:T(8,128)} %bitcast.28, f32[64,32]{0,1:T(8,128)S(1)} %psum.22), kind=kOutput, calls=%fused_computation.78 | convolution fusion | flops 1358956544 | bytes 21241856 | tf_op jit(solution)/shard_map/dot_general | solution.py:43
  216.4 66.5 %reduce-scatter.2.cloned.1.call-done = f32[8,55296]{1,0:T(8,128)} async-done(((f32[32,55296]{1,0:T(8,128)}), f32[8,55296]{1,0:T(8,128)}) %reduce-scatter.2.cloned.1.call-update) | async-done | bytes 1769488 | tf_op jit(solution)/shard_map/reduce_scatter | solution.py:61
  282.9 2.9 sub.3
  285.8 72.1 %all-gather.5.cloned.1.call-done = f32[32,55296]{1,0:T(8,128)} async-done(((f32[8,55296]{1,0:T(8,128)}), f32[32,55296]{1,0:T(8,128)}) %all-gather.5.cloned.1.call-update) | async-done | bytes 7077904 | tf_op jit(solution)/shard_map/all_gather | solution.py:65
  357.9 9.1 %fusion.49 = f32[32,32]{0,1:T(8,128)S(1)} fusion(f32[32,55296]{1,0:T(8,128)} %all-gather.5.cloned.1.call-done), kind=kOutput, calls=%fused_computation.91 | convolution fusion | flops 679477248 | bytes 7081984 | tf_op jit(solution)/shard_map/dot_general | solution.py:43
  367.0 128.5 %psum.23 = f32[32,32]{0,1:T(8,128)S(1)} all-reduce(f32[32,32]{0,1:T(8,128)S(1)} %fusion.49), channel_id=1, replica_groups=mesh['gx'=8,'gy'=4,'band'=4] {'gx','gy'}, use_global_device_ids=true, to_apply=%region_3.4 | all-reduce | flops 1024 | bytes 8192 | tf_op jit(solution)/shard_map/psum | solution.py:66
  495.6 2.9 cholesky.17
  499.9 2.4 custom-call.6
  502.5 6.5 %fusion.43 = f32[8,55296]{1,0:T(8,128)} fusion(f32[32,55296]{1,0:T(8,128)} %all-gather.5.cloned.1.call-done, f32[32,32]{1,0:T(8,128)S(1)} %fusion.37, s32[]{:T(128)S(6)} %select_n.8), kind=kOutput, calls=%fused_computation.84 | convolution fusion | flops 169869312 | bytes 8851460 | tf_op jit(solution)/shard_map/dot_general | solution.py:43
  (33 shorter events, 6.6 us)
Async XLA Ops:
  6.5 142.9 %all-gather.3.cloned.1.call-start = ((), (), s32[]{:S(2)}) async-start(), calls=%async_computation.1 | async-start | bytes 8847360 | tf_op jit(solution)/shard_map/all_gather | solution.py:59
  8.5 3.5 copy-start.2
  8.7 3.2 collective-permute-start.1
  10.0 5.9 %collective-permute-start = (f32[8,4,24,192]{3,2,0,1:T(8,128)S(1)}, f32[8,4,24,192]{3,2,0,1:T(8,128)S(1)}, u32[]{:S(2)}, u32[]{:S(2)}) collective-permute-start(f32[8,4,24,192]{3,2,0,1:T(8,128)S(1)} %get-tuple-element.10), channel_id=1, source_target_pairs={{16,0},{32,16},{48,32},{64,48},{80,64},{96,80},{112,96},{17,1},{33... | collective-permute-start | bytes 1769480 | tf_op jit(solution)/shard_map/ppermute | solution.py:18
  12.9 3.5 copy-start.1
  16.1 17.1 %copy-start = (f32[8,16,24,192]{3,2,0,1:T(8,128)}, f32[8,16,24,192]{3,2,0,1:T(8,128)S(1)}, u32[]{:S(2)}) copy-start(f32[8,16,24,192]{3,2,0,1:T(8,128)S(1)} %get-tuple-element.12) | copy-start | bytes 7077892
  16.1 17.1 %copy-start.3 = (f32[8,20,24,192]{3,2,0,1:T(8,128)}, f32[8,20,24,192]{3,2,0,1:T(8,128)S(1)}, u32[]{:S(2)}) copy-start(f32[8,20,24,192]{3,2,0,1:T(8,128)S(1)} %get-tuple-element.13) | copy-start | bytes 8847364
  16.4 12.5 %collective-permute-start.2 = (f32[8,20,4,192]{3,2,0,1:T(4,128)S(1)}, f32[8,20,4,192]{3,2,0,1:T(4,128)S(1)}, u32[]{:S(2)}, u32[]{:S(2)}) collective-permute-start(f32[8,20,4,192]{3,2,0,1:T(4,128)S(1)} %get-tuple-element.5), channel_id=1, source_target_pairs={{4,0},{8,4},{12,8},{5,1},{9,5},{13,9},{6,2},{10,6},{14,10},{7,3},{... | collective-permute-start | bytes 1474568 | tf_op jit(solution)/shard_map/ppermute | solution.py:18
  17.7 12.6 %collective-permute-start.3 = (f32[8,20,4,192]{3,2,0,1:T(4,128)S(1)}, f32[8,20,4,192]{3,2,0,1:T(4,128)S(1)}, u32[]{:S(2)}, u32[]{:S(2)}) collective-permute-start(f32[8,20,4,192]{3,2,0,1:T(4,128)S(1)} %get-tuple-element.6), channel_id=1, source_target_pairs={{0,4},{4,8},{8,12},{1,5},{5,9},{9,13},{2,6},{6,10},{10,14},{3,7},{... | collective-permute-start | bytes 1474568 | tf_op jit(solution)/shard_map/ppermute | solution.py:17
  53.9 2.3 copy-start.5
  58.6 224.3 %reduce-scatter.2.cloned.1.call-start = ((), (), s32[]{:S(2)}) async-start(), calls=%async_computation.2 | async-start | bytes 8847360 | tf_op jit(solution)/shard_map/reduce_scatter | solution.py:61
  216.3 66.6 %copy-start.4 = (f32[8,12,4608]{2,0,1:T(8,128)S(1)}, f32[8,12,4608]{2,0,1:T(8,128)}, u32[]{:S(2)}) copy-start(f32[8,12,4608]{2,0,1:T(8,128)} %multiply_add_fusion) | copy-start | bytes 5308420
  216.3 141.6 %all-gather.5.cloned.1.call-start = ((), (), s32[]{:S(2)}) async-start(), calls=%async_computation.3 | async-start | bytes 8847360 | tf_op jit(solution)/shard_map/all_gather | solution.py:65
Sparse Core Ops, SparseCore 0:
  58.8 90.6 all-gather.2
  216.4 66.4 reduce-scatter.1
  285.9 71.9 all-gather.4
